TPU v7x, 32 devices: a whole 2x2x4 slice. The times are simulated.
32 devices in a mesh: row: 4 (over y, x), col: 8 (over z, core).
Axes of the slice: x: 2, y: 2, z: 4, core: 2. Of those that a mesh axis runs over, the one named last changes fastest.
Arguments:
- stiffness: float32 [12, 4, 128, 6144], P(None, 'row', None, 'col'), may hold values from -8 to 8
- lower_first: float32 [1024, 10, 4, 128], P('col', None, 'row'), may hold values from -0.1875 to 0.1875
- lower_second: float32 [1024, 8, 4, 128], P('col', None, 'row'), may hold values from -0.1875 to 0.1875
- diag_inv: float32 [2, 1024, 2, 4, 128], P(None, 'col', None, 'row'), as said below
Outputs:
- reduced: float32 [12, 4, 128, 6144], P(None, 'row', None, 'col')
Inputs may be any that keep to these rules, and one draw needn't show every extreme that they name: Each block of diag_inv, read as a 1024 x 1024 matrix, is zero above its diagonal and has a positive diagonal.
All inputs are finite; a program needn't handle non-finite values.
Results may differ from a plain program's by a relative error of at most 0.000086.
Values sent between devices are 32-bit elements; how exact they have to be, the bound alone decides.
A program may use at most 128 MiB of HBM per device.

v0:
```python
import jax
import jax.numpy as jnp
from jax import lax
from jax.sharding import PartitionSpec as P


def product(left, right):
    return jnp.dot(left, right, precision=lax.Precision.HIGH, preferred_element_type=jnp.float32)


def apply_cols(columns, factor):
    return lax.dot_general(
        columns,
        factor,
        (((0,), (0,)), ((), ())),
        precision=lax.Precision.HIGH,
        preferred_element_type=jnp.float32,
    )


def shards(stiffness, lower_first, lower_second, diag_inv):
    cycles = stiffness.shape[0]
    rblk = stiffness.shape[2]
    cdev = stiffness.shape[3]
    pcount = diag_inv.shape[2]
    nrow = lax.axis_size("row")
    nb = diag_inv.shape[1] * lax.axis_size("col")
    height = pcount * rblk
    matrix_rows = stiffness.reshape(cycles * rblk, cdev)
    inv_cols = lax.all_gather(diag_inv, "col", axis=1, tiled=True)
    inverse = inv_cols.reshape(2, nb, height)

    def own_rows(solved):
        grouped = solved.reshape(pcount, nrow, rblk, cdev)
        mine = lax.dynamic_slice_in_dim(grouped, lax.axis_index("row"), 1, 1)
        return mine.reshape(height, cdev)

    w_first = lax.psum(product(inverse[0], matrix_rows[:height]), "row")
    coupling = lax.all_gather(lower_first[:, :pcount], "col", axis=0, tiled=True).reshape(
        nb, height
    )
    w_second = lax.psum(
        product(inverse[1], matrix_rows[height : 2 * height] - apply_cols(coupling, w_first)), "row"
    )
    pieces = (
        lax.all_gather(lower_first[:, pcount:], "col", axis=0, tiled=True),
        lax.all_gather(lower_second, "col", axis=0, tiled=True),
    )
    count = pieces[0].shape[0]
    first_piece = pieces[0].reshape(count, -1)
    second_piece = pieces[1].reshape(count, -1)
    remain = (
        matrix_rows[2 * height :]
        - apply_cols(first_piece, w_first)
        - apply_cols(second_piece, w_second)
    )
    stacked = jnp.concatenate([own_rows(w_first), own_rows(w_second), remain], axis=0)
    return stacked.reshape(cycles, 1, rblk, cdev)


def solution(mesh):
    placed = (
        P(None, "row", None, "col"),
        P("col", None, "row", None),
        P("col", None, "row", None),
        P(None, "col", None, "row", None),
    )
    return jax.shard_map(
        shards, mesh=mesh, in_specs=placed, out_specs=P(None, "row", None, "col"), check_vma=False
    )
```

profile of v0, /device:TPU:0, one launch (start us, length us, event | category | flops | bytes accessed | tf_op | source)
XLA Modules:
  0.0 369.2 jit_solution(9611690720741950493)
XLA Ops:
  6.5 0.0 all-gather.5.cloned.1.call-start
  6.5 0.7 all-gather.5.cloned.1.call-update
  7.3 0.0 all-gather.7.cloned.1.call-start
  7.3 1.6 slice.37
  8.9 0.0 all-gather.7.cloned.1.call-update
  8.9 0.0 all-reduce.3.cloned.1.call-start
  8.9 1.5 fusion.16
  10.4 30.4 %all-gather.5.cloned.1.call-done = f32[2,1024,2,1,128]{4,3,2,1,0:T(1,128)} async-done(((f32[2,128,2,1,128]{4,3,2,1,0:T(1,128)}), f32[2,1024,2,1,128]{4,3,2,1,0:T(1,128)}) %all-gather.5.cloned.1.call-update) | async-done | bytes 2097168 | tf_op jit(solution)/shard_map/all_gather | solution.py:30
  40.8 7.8 %slice_reduce_fusion = (f32[1024,2,128]{2,1,0:T(2,128)S(1)}, f32[1024,2,128]{2,1,0:T(2,128)S(1)}) fusion(f32[2,1024,2,1,128]{4,3,2,1,0:T(1,128)} %all-gather.5.cloned.1.call-done), kind=kLoop, calls=%fused_computation.19 | loop fusion | bytes 4194304 | tf_op jit(solution)/shard_map/slice | solution.py:43
  48.7 3.1 fusion.13
  51.8 0.0 all-reduce.3.cloned.1.call-update
  51.8 0.0 all-reduce.5.cloned.1.call-start
  51.9 0.3 copy.21
  52.2 12.0 %all-gather.7.cloned.1.call-done = f32[1024,2,1,128]{3,1,2,0:T(2,128)} async-done(((f32[128,2,1,128]{3,1,2,0:T(2,128)}), f32[1024,2,1,128]{3,1,2,0:T(2,128)}) %all-gather.7.cloned.1.call-update) | async-done | bytes 1048592 | tf_op jit(solution)/shard_map/all_gather | solution.py:39
  64.1 89.7 %all-reduce.3.cloned.1.call-done = f32[1024,768]{1,0:T(8,128)} async-done(((f32[1024,768]{1,0:T(8,128)}), f32[1024,768]{1,0:T(8,128)}) %all-reduce.3.cloned.1.call-update) | async-done | bytes 3145744 | tf_op jit(solution)/shard_map/psum | solution.py:38
  153.8 4.8 %fusion.8 = f32[256,768]{0,1:T(8,128)S(1)} fusion(f32[256,768]{0,1:T(8,128)S(1)} %copy.21, f32[1024,768]{1,0:T(8,128)} %all-reduce.3.cloned.1.call-done, f32[128,8,2,128]{3,2,1,0:T(2,128)} %bitcast.76), kind=kOutput, calls=%fused_computation.11 | convolution fusion | flops 1208156160 | bytes 5767168 | tf_op jit(solution)/shard_map/dot_general | solution.py:12
  158.6 0.0 copy-start.3
  158.6 3.1 convolution_bitcast_fusion
  161.7 0.0 all-reduce.5.cloned.1.call-update
  161.7 0.0 all-gather.11.cloned.1.call-start
  161.8 0.5 all-gather.11.cloned.1.call-update
  162.3 0.2 all-gather.9.cloned.1.call-start
  162.5 0.0 copy-done.3
  162.6 0.8 slice.41
  163.4 0.0 all-gather.9.cloned.1.call-update
  163.4 3.8 %slice.39 = f32[8,1,128,768]{3,2,1,0:T(8,128)} slice(f32[12,1,128,768]{3,2,1,0:T(8,128)} %param.4), slice={[4:12], [0:1], [0:128], [0:768]} | slice | bytes 6291456 | tf_op jit(solution)/shard_map/slice | solution.py:53
  167.2 0.0 copy-start
  167.2 4.1 %copy.22 = f32[1024,768]{0,1:T(8,128)} copy(f32[1024,768]{1,0:T(8,128)} %bitcast.65) | data formatting | bytes 6291456 | tf_op jit(solution)/shard_map/slice | solution.py:53
  171.3 0.0 copy-done
  171.3 0.9 constant_dynamic-slice_fusion
  172.3 2.3 copy.20
  174.6 74.3 %all-reduce.5.cloned.1.call-done = f32[1024,768]{0,1:T(8,128)} async-done(((f32[1024,768]{0,1:T(8,128)}), f32[1024,768]{0,1:T(8,128)}) %all-reduce.5.cloned.1.call-update) | async-done | bytes 3145744 | tf_op jit(solution)/shard_map/psum | solution.py:42
  248.8 5.1 %reshape.36 = f32[2,4,128,768]{2,1,0,3:T(4,128)} reshape(f32[1024,768]{0,1:T(8,128)} %all-reduce.5.cloned.1.call-done) | data formatting | bytes 6291456 | tf_op jit(solution)/shard_map/reshape | solution.py:34
  254.0 4.6 %dynamic-slice_reduce_fusion = f32[2,128,768]{1,0,2:T(2,128)S(1)} fusion(f32[2,4,128,768]{2,1,0,3:T(4,128)} %reshape.36, s32[]{:T(128)S(6)} %select_n.4), kind=kLoop, calls=%fused_computation.22 | loop fusion | bytes 1572868 | tf_op jit(solution)/shard_map/dynamic_slice | solution.py:35
  258.5 0.9 copy.54
  259.5 37.7 %all-gather.11.cloned.1.call-done = f32[1024,8,1,128]{3,1,2,0:T(8,128)} async-done(((f32[128,8,1,128]{3,1,2,0:T(8,128)}), f32[1024,8,1,128]{3,1,2,0:T(8,128)}) %all-gather.11.cloned.1.call-update) | async-done | bytes 4194320 | tf_op jit(solution)/shard_map/all_gather | solution.py:47
  297.2 9.6 %fusion = f32[768,1024]{1,0:T(8,128)} fusion(f32[1024,768]{0,1:T(8,128)} %all-reduce.5.cloned.1.call-done, f32[128,8,8,128]{3,2,1,0:T(8,128)} %bitcast.66), kind=kOutput, calls=%fused_computation.1 | convolution fusion | flops 4831838208 | bytes 10485760 | tf_op jit(solution)/shard_map/dot_general | solution.py:12
  306.8 37.6 %all-gather.9.cloned.1.call-done = f32[1024,8,1,128]{3,1,2,0:T(8,128)} async-done(((f32[128,8,1,128]{3,1,2,0:T(8,128)}), f32[1024,8,1,128]{3,1,2,0:T(8,128)}) %all-gather.9.cloned.1.call-update) | async-done | bytes 4194320 | tf_op jit(solution)/shard_map/all_gather | solution.py:46
  344.3 0.0 copy-start.1
  344.3 0.0 copy-start.2
  344.3 9.4 %bitcast_subtract_fusion = f32[1024,768]{0,1:T(8,128)S(1)} fusion(f32[768,1024]{1,0:T(8,128)} %fusion, f32[1024,768]{0,1:T(8,128)} %copy.22, f32[1024,768]{1,0:T(8,128)S(1)} %copy-done, f32[128,8,8,128]{3,2,1,0:T(8,128)} %bitcast.69), kind=kOutput, calls=%fused_computation.7 | convolution fusion | flops 4833411072 | bytes 16777216 | tf_op jit(solution)/shard_map/dot_general | solution.py:12
  353.7 0.0 copy-done.1
  353.8 0.0 copy-done.2
  353.8 2.6 pad_maximum_fusion
  356.4 6.0 %copy.18 = f32[1536,768]{1,0:T(8,128)} copy(f32[1536,768]{0,1:T(8,128)} %pad_maximum_fusion) | data formatting | bytes 9437184 | tf_op jit(solution)/shard_map/concatenate | solution.py:57
Async XLA Ops:
  6.5 34.3 %all-gather.5.cloned.1.call-start = ((), (), s32[]{:S(2)}) async-start(), calls=%async_computation | async-start | bytes 2359296 | tf_op jit(solution)/shard_map/all_gather | solution.py:30
  7.3 56.9 %all-gather.7.cloned.1.call-start = ((), (), s32[]{:S(2)}) async-start(), calls=%async_computation.2 | async-start | bytes 1179648 | tf_op jit(solution)/shard_map/all_gather | solution.py:39
  8.9 144.9 %all-reduce.3.cloned.1.call-start = ((), (), s32[]{:S(2)}) async-start(), calls=%async_computation.1 | async-start | bytes 6291456 | tf_op jit(solution)/shard_map/psum | solution.py:38
  51.8 197.0 %all-reduce.5.cloned.1.call-start = ((), (), s32[]{:S(2)}) async-start(), calls=%async_computation.3 | async-start | bytes 6291456 | tf_op jit(solution)/shard_map/psum | solution.py:42
  158.6 4.0 %copy-start.3 = (f32[128,10,1,128]{3,2,1,0:T(1,128)S(1)}, f32[128,10,1,128]{3,2,1,0:T(1,128)}, u32[]{:S(2)}) copy-start(f32[128,10,1,128]{3,2,1,0:T(1,128)} %param.5) | copy-start | bytes 1966084
  161.7 135.4 %all-gather.11.cloned.1.call-start = ((), (), s32[]{:S(2)}) async-start(), calls=%async_computation.5 | async-start | bytes 4718592 | tf_op jit(solution)/shard_map/all_gather | solution.py:47
  162.3 182.0 %all-gather.9.cloned.1.call-start = ((), (), s32[]{:S(2)}) async-start(), calls=%async_computation.4 | async-start | bytes 4718592 | tf_op jit(solution)/shard_map/all_gather | solution.py:46
  167.2 4.1 %copy-start = (f32[1024,768]{1,0:T(8,128)S(1)}, f32[1024,768]{1,0:T(8,128)}, u32[]{:S(2)}) copy-start(f32[1024,768]{1,0:T(8,128)} %all-reduce.3.cloned.1.call-done) | copy-start | bytes 9437188
  344.3 9.4 %copy-start.1 = (f32[256,768]{0,1:T(8,128)S(1)}, f32[256,768]{0,1:T(8,128)}, u32[]{:S(2)}) copy-start(f32[256,768]{0,1:T(8,128)} %copy.20) | copy-start | bytes 2359300
  344.3 9.4 %copy-start.2 = (f32[96,8,2,128]{3,1,2,0:T(8,128)S(1)}, f32[96,8,2,128]{3,1,2,0:T(8,128)}, u32[]{:S(2)}) copy-start(f32[96,8,2,128]{3,1,2,0:T(8,128)} %copy.54) | copy-start | bytes 2359300
Sparse Core Ops, SparseCore 0:
  8.9 31.8 all-gather.4
  42.4 21.6 all-gather.6
  67.2 86.5 all-reduce.2
  161.9 86.9 all-reduce.4
  250.3 46.8 all-gather.10
  298.6 45.6 all-gather.8
where the time goes:
time: 370 us; the launch traced here: 369 us
  waiting for transfers between devices  283 us (76%)
  local copies, waits for them, and re-layouts  39.8 us (11%)
  matrix products  30 us (8%)
  between operations  13.6 us (4%)
    psum x1, waiting for transfers between devices, shards(): w_first = lax.psum(product(inverse[0], matrix_rows[:height]), 'row')  89.7 us
    psum x1, waiting for transfers between devices, shards(): lax.psum(product(inverse[1], matrix_rows[height:2 * height] - apply_cols(...  74.3 us
    all_gather x1, waiting for transfers between devices, shards(): lax.all_gather(lower_second, 'col', axis=0, tiled=True)  37.7 us
    all_gather x1, waiting for transfers between devices, shards(): lax.all_gather(lower_first[:, pcount:], 'col', axis=0, tiled=True)  37.6 us
    all_gather x1, waiting for transfers between devices, shards(): inv_cols = lax.all_gather(diag_inv, 'col', axis=1, tiled=True)  30.4 us
    dot_general x3, matrix products, apply_cols(): lax.dot_general(columns, factor, (((0,), (0,)), ((), ())), precision=lax....  23.8 us
    all_gather x1, waiting for transfers between devices, shards(): lax.all_gather(lower_first[:, :pcount], 'col', axis=0, tiled=True)  12 us
    slice x2, local copies, waits for them, and re-layouts, shards(): matrix_rows[2 * height:] - apply_cols(first_piece, w_first)  7.89 us
  transfers between devices with their start and end apart: 6, of which 6 were waited for; matrix products, arithmetic and copies ran while one was open for 13% of the time, Pallas kernels for 0%

commit v1 on v0

--- a/solution.py
+++ b/solution.py
@@ -2,6 +2,13 @@
 import jax.numpy as jnp
 from jax import lax
 from jax.sharding import PartitionSpec as P
+
+
+def exchange_gather(x, axis, dim):
+    peers = lax.axis_size(axis)
+    blocks = jnp.stack([x for _ in range(peers)])
+    blocks = lax.all_to_all(blocks, axis, split_axis=0, concat_axis=0)
+    return jnp.concatenate(blocks, axis=dim)
 
 
 def product(left, right):
@@ -27,7 +34,7 @@
     nb = diag_inv.shape[1] * lax.axis_size("col")
     height = pcount * rblk
     matrix_rows = stiffness.reshape(cycles * rblk, cdev)
-    inv_cols = lax.all_gather(diag_inv, "col", axis=1, tiled=True)
+    inv_cols = exchange_gather(diag_inv, "col", 1)
     inverse = inv_cols.reshape(2, nb, height)
 
     def own_rows(solved):

time: 370 us -> 311 us (0.84)
  waiting for transfers between devices: 283 us -> 213 us
  starting transfers between devices: 0.39 us -> 6.74 us
  local copies, waits for them, and re-layouts: 39.8 us -> 43.8 us
    all_to_all x0 -> x1, waiting for transfers between devices: none -> 53 us  [exchange_gather(): blocks = lax.all_to_all(blocks, axis, split_axis=0, concat_axis=0)]
    all_gather x1, waiting for transfers between devices: 37.7 us -> 0.01 us  [shards(): lax.all_gather(lower_second, 'col', axis=0, tiled=True)]
    all_gather x1, waiting for transfers between devices: 37.6 us -> 0.01 us  [shards(): lax.all_gather(lower_first[:, pcount:], 'col', axis=0, tiled=True)]
    all_gather x1 -> x0, waiting for transfers between devices: 30.4 us -> none  [shards(): inv_cols = lax.all_gather(diag_inv, 'col', axis=1, tiled=True)]
    all_gather x1, waiting for transfers between devices: 12 us -> 0.02 us  [shards(): lax.all_gather(lower_first[:, :pcount], 'col', axis=0, tiled=True)]
    all_to_all x0 -> x1, starting transfers between devices: none -> 6.35 us  [exchange_gather(): blocks = lax.all_to_all(blocks, axis, split_axis=0, concat_axis=0)]
    psum x1, waiting for transfers between devices: 89.7 us -> 85.3 us  [shards(): w_first = lax.psum(product(inverse[0], matrix_rows[:height]), 'row')]
    another operation x0 -> x1, local copies, waits for them, and re-layouts: none -> 3.88 us  [exchange_gather(): blocks = jnp.stack([x for _ in range(peers)])]
  transfers between devices with their start and end apart: 6 -> 6, of which waited for: 6 -> 3; matrix products, arithmetic and copies ran while one was open for 13% -> 15% of each run, Pallas kernels for 0% -> 0%
where the time goes in v1:
time: 311 us
  waiting for transfers between devices  213 us (68%)
  local copies, waits for them, and re-layouts  43.8 us (14%)
  matrix products  30 us (10%)
  between operations  14.7 us (5%)
  starting transfers between devices  6.74 us (2%)
    psum x1, waiting for transfers between devices, shards(): w_first = lax.psum(product(inverse[0], matrix_rows[:height]), 'row')  85.3 us
    psum x1, waiting for transfers between devices, shards(): lax.psum(product(inverse[1], matrix_rows[height:2 * height] - apply_cols(...  73.7 us
    all_to_all x1, waiting for transfers between devices, exchange_gather(): blocks = lax.all_to_all(blocks, axis, split_axis=0, concat_axis=0)  53 us
    dot_general x3, matrix products, apply_cols(): lax.dot_general(columns, factor, (((0,), (0,)), ((), ())), precision=lax....  23.8 us
    slice x2, local copies, waits for them, and re-layouts, shards(): matrix_rows[2 * height:] - apply_cols(first_piece, w_first)  7.83 us
    slice x1, local copies, waits for them, and re-layouts, shards(): inverse[1]  6.6 us
    all_to_all x1, starting transfers between devices, exchange_gather(): blocks = lax.all_to_all(blocks, axis, split_axis=0, concat_axis=0)  6.35 us
  transfers between devices with their start and end apart: 6, of which 3 were waited for; matrix products, arithmetic and copies ran while one was open for 15% of the time, Pallas kernels for 0%

profile of v1, /device:TPU:0, one launch (start us, length us, event | category | flops | bytes accessed | tf_op | source)
XLA Modules:
  0.0 310.8 jit_solution(15696055227488575447)
XLA Ops:
  7.4 3.9 %stack.2 = f32[8,2,128,2,1,128]{5,4,3,2,1,0:T(1,128)} broadcast(f32[2,128,2,128]{3,2,1,0:T(2,128)} %bitcast.84), dimensions={1,2,3,5} | broadcast | bytes 2359296 | tf_op jit(solution)/shard_map/stack | solution.py:9
  11.3 6.4 %all-to-all-start = ((f32[8,2,128,2,1,128]{5,4,3,2,1,0:T(1,128)}), f32[8,2,128,2,1,128]{5,4,3,2,1,0:T(1,128)S(1)}, u32[]{:S(2)}, u32[]{:S(2)}) async-start(f32[8,2,128,2,1,128]{5,4,3,2,1,0:T(1,128)} %stack.2), calls=%async_computation | async-start | bytes 4194304 | tf_op jit(solution)/shard_map/all_to_all | solution.py:10
  17.6 0.0 all-gather.4.cloned.1.call-start
  17.7 1.6 slice.37
  19.2 0.0 all-gather.4.cloned.1.call-update
  19.2 0.0 all-reduce.3.cloned.1.call-start
  19.3 2.7 fusion.16
  22.0 53.0 %all-to-all-done = f32[8,2,128,2,1,128]{5,4,3,2,1,0:T(1,128)S(1)} async-done(((f32[8,2,128,2,1,128]{5,4,3,2,1,0:T(1,128)}), f32[8,2,128,2,1,128]{5,4,3,2,1,0:T(1,128)S(1)}, u32[]{:S(2)}, u32[]{:S(2)}) %all-to-all-start) | async-done | bytes 2097184 | tf_op jit(solution)/shard_map/all_to_all | solution.py:10
  75.1 0.0 copy-start.3
  75.1 6.6 %slice_reduce_fusion = (f32[8,128,2,128]{3,2,1,0:T(2,128)S(1)}, f32[8,128,2,128]{3,2,1,0:T(2,128)S(1)}) fusion(f32[2,8,128,2,1,128]{5,4,3,2,0,1:T(1,128)S(1)} %bitcast.70), kind=kLoop, calls=%fused_computation.19 | loop fusion | bytes 4194304 | tf_op jit(solution)/shard_map/slice | solution.py:50
  81.7 0.0 copy-done.3
  81.7 0.0 copy-start.4
  81.7 3.1 %fusion.13 = f32[1024,768]{1,0:T(8,128)} fusion(f32[256,768]{1,0:T(8,128)S(1)} %bitcast.76, f32[128,8,2,128]{3,2,1,0:T(2,128)S(1)} %bitcast.73), kind=kOutput, calls=%fused_computation.16 | convolution fusion | flops 1207959552 | bytes 4980736 | tf_op jit(solution)/shard_map/dot_general | solution.py:15
  84.8 0.0 all-reduce.3.cloned.1.call-update
  84.8 0.0 all-reduce.5.cloned.1.call-start
  84.9 0.0 copy-done.4
  84.9 0.3 copy.21
  85.2 0.0 all-gather.4.cloned.1.call-done
  85.2 85.3 %all-reduce.3.cloned.1.call-done = f32[1024,768]{1,0:T(8,128)} async-done(((f32[1024,768]{1,0:T(8,128)}), f32[1024,768]{1,0:T(8,128)}) %all-reduce.3.cloned.1.call-update) | async-done | bytes 3145744 | tf_op jit(solution)/shard_map/psum | solution.py:45
  170.5 4.8 %fusion.8 = f32[256,768]{0,1:T(8,128)S(1)} fusion(f32[256,768]{0,1:T(8,128)S(1)} %copy.21, f32[1024,768]{1,0:T(8,128)} %all-reduce.3.cloned.1.call-done, f32[128,8,2,128]{3,2,1,0:T(2,128)} %bitcast.81), kind=kOutput, calls=%fused_computation.11 | convolution fusion | flops 1208156160 | bytes 5767168 | tf_op jit(solution)/shard_map/dot_general | solution.py:19
  175.3 0.0 copy-start.5
  175.4 3.1 %convolution_bitcast_fusion = f32[1024,768]{0,1:T(8,128)} fusion(f32[256,768]{0,1:T(8,128)S(1)} %fusion.8, f32[128,8,2,128]{3,2,1,0:T(2,128)S(1)} %bitcast.72), kind=kOutput, calls=%fused_computation.9 | convolution fusion | flops 1207959552 | bytes 4980736 | tf_op jit(solution)/shard_map/dot_general | solution.py:15
  178.5 0.0 all-reduce.5.cloned.1.call-update
  178.5 0.0 all-gather.8.cloned.1.call-start
  178.5 0.7 all-gather.8.cloned.1.call-update
  179.2 0.2 all-gather.6.cloned.1.call-start
  179.5 0.0 copy-done.5
  179.5 0.8 slice.41
  180.3 0.0 all-gather.6.cloned.1.call-update
  180.3 3.8 %slice.39 = f32[8,1,128,768]{3,2,1,0:T(8,128)} slice(f32[12,1,128,768]{3,2,1,0:T(8,128)} %param.4), slice={[4:12], [0:1], [0:128], [0:768]} | slice | bytes 6291456 | tf_op jit(solution)/shard_map/slice | solution.py:60
  184.1 0.0 copy-start
  184.1 4.1 %copy.22 = f32[1024,768]{0,1:T(8,128)} copy(f32[1024,768]{1,0:T(8,128)} %bitcast.69) | data formatting | bytes 6291456 | tf_op jit(solution)/shard_map/slice | solution.py:60
  188.2 0.0 copy-done
  188.2 1.0 constant_dynamic-slice_fusion
  189.2 2.3 copy.20
  191.5 73.7 %all-reduce.5.cloned.1.call-done = f32[1024,768]{0,1:T(8,128)} async-done(((f32[1024,768]{0,1:T(8,128)}), f32[1024,768]{0,1:T(8,128)}) %all-reduce.5.cloned.1.call-update) | async-done | bytes 3145744 | tf_op jit(solution)/shard_map/psum | solution.py:49
  265.3 5.1 %reshape.42 = f32[2,4,128,768]{2,1,0,3:T(4,128)} reshape(f32[1024,768]{0,1:T(8,128)} %all-reduce.5.cloned.1.call-done) | data formatting | bytes 6291456 | tf_op jit(solution)/shard_map/reshape | solution.py:41
  270.4 4.6 %dynamic-slice_reduce_fusion = f32[2,128,768]{1,0,2:T(2,128)S(1)} fusion(f32[2,4,128,768]{2,1,0,3:T(4,128)} %reshape.42, s32[]{:T(128)S(6)} %select_n.4), kind=kLoop, calls=%fused_computation.22 | loop fusion | bytes 1572868 | tf_op jit(solution)/shard_map/dynamic_slice | solution.py:42
  275.0 1.0 copy.54
  275.9 0.0 all-gather.8.cloned.1.call-done
  275.9 9.6 %fusion = f32[768,1024]{1,0:T(8,128)} fusion(f32[1024,768]{0,1:T(8,128)} %all-reduce.5.cloned.1.call-done, f32[128,8,8,128]{3,2,1,0:T(8,128)} %bitcast.71), kind=kOutput, calls=%fused_computation.1 | convolution fusion | flops 4831838208 | bytes 10485760 | tf_op jit(solution)/shard_map/dot_general | solution.py:19
  285.5 0.0 all-gather.6.cloned.1.call-done
  285.6 0.0 copy-start.1
  285.6 9.4 %bitcast_subtract_fusion = f32[1024,768]{0,1:T(8,128)S(1)} fusion(f32[768,1024]{1,0:T(8,128)} %fusion, f32[1024,768]{0,1:T(8,128)} %copy.22, f32[1024,768]{1,0:T(8,128)S(1)} %copy-done, f32[128,8,8,128]{3,2,1,0:T(8,128)} %bitcast.74), kind=kOutput, calls=%fused_computation.7 | convolution fusion | flops 4833411072 | bytes 16777216 | tf_op jit(solution)/shard_map/dot_general | solution.py:19
  295.0 0.0 copy-done.1
  295.0 0.0 copy-done.2
  295.0 2.6 pad_maximum_fusion
  297.6 6.0 %copy.18 = f32[1536,768]{1,0:T(8,128)} copy(f32[1536,768]{0,1:T(8,128)} %pad_maximum_fusion) | data formatting | bytes 9437184 | tf_op jit(solution)/shard_map/concatenate | solution.py:64
  (1 shorter events, 0.0 us)
Async XLA Ops:
  11.3 63.8 %all-to-all-start = ((f32[8,2,128,2,1,128]{5,4,3,2,1,0:T(1,128)}), f32[8,2,128,2,1,128]{5,4,3,2,1,0:T(1,128)S(1)}, u32[]{:S(2)}, u32[]{:S(2)}) async-start(f32[8,2,128,2,1,128]{5,4,3,2,1,0:T(1,128)} %stack.2), calls=%async_computation | async-start | bytes 4194304 | tf_op jit(solution)/shard_map/all_to_all | solution.py:10
  17.6 67.6 %all-gather.4.cloned.1.call-start = ((), (), s32[]{:S(2)}) async-start(), calls=%async_computation.2 | async-start | bytes 1179648 | tf_op jit(solution)/shard_map/all_gather | solution.py:46
  19.2 151.3 %all-reduce.3.cloned.1.call-start = ((), (), s32[]{:S(2)}) async-start(), calls=%async_computation.1 | async-start | bytes 6291456 | tf_op jit(solution)/shard_map/psum | solution.py:45
  75.1 6.6 %copy-start.3 = (f32[2,1,128,768]{3,2,1,0:T(8,128)S(1)}, f32[2,1,128,768]{3,2,1,0:T(8,128)}, u32[]{:S(2)}) copy-start(f32[2,1,128,768]{3,2,1,0:T(8,128)} %get-tuple-element.7) | copy-start | bytes 2359300
  81.7 3.2 %copy-start.4 = (f32[2,1,128,768]{3,2,1,0:T(8,128)S(1)}, f32[2,1,128,768]{3,2,1,0:T(8,128)}, u32[]{:S(2)}) copy-start(f32[2,1,128,768]{3,2,1,0:T(8,128)} %get-tuple-element.8) | copy-start | bytes 2359300
  84.8 180.4 %all-reduce.5.cloned.1.call-start = ((), (), s32[]{:S(2)}) async-start(), calls=%async_computation.3 | async-start | bytes 6291456 | tf_op jit(solution)/shard_map/psum | solution.py:49
  175.3 4.1 %copy-start.5 = (f32[128,10,1,128]{3,2,1,0:T(1,128)S(1)}, f32[128,10,1,128]{3,2,1,0:T(1,128)}, u32[]{:S(2)}) copy-start(f32[128,10,1,128]{3,2,1,0:T(1,128)} %param.5) | copy-start | bytes 1966084
  178.5 97.5 %all-gather.8.cloned.1.call-start = ((), (), s32[]{:S(2)}) async-start(), calls=%async_computation.5 | async-start | bytes 4718592 | tf_op jit(solution)/shard_map/all_gather | solution.py:54
  179.2 106.3 %all-gather.6.cloned.1.call-start = ((), (), s32[]{:S(2)}) async-start(), calls=%async_computation.4 | async-start | bytes 4718592 | tf_op jit(solution)/shard_map/all_gather | solution.py:53
  184.1 4.1 %copy-start = (f32[1024,768]{1,0:T(8,128)S(1)}, f32[1024,768]{1,0:T(8,128)}, u32[]{:S(2)}) copy-start(f32[1024,768]{1,0:T(8,128)} %all-reduce.3.cloned.1.call-done) | copy-start | bytes 9437188
  285.6 9.4 %copy-start.1 = (f32[256,768]{0,1:T(8,128)S(1)}, f32[256,768]{0,1:T(8,128)}, u32[]{:S(2)}) copy-start(f32[256,768]{0,1:T(8,128)} %copy.20) | copy-start | bytes 2359300
  285.6 9.4 %copy-start.2 = (f32[96,8,2,128]{3,1,2,0:T(8,128)S(1)}, f32[96,8,2,128]{3,1,2,0:T(8,128)}, u32[]{:S(2)}) copy-start(f32[96,8,2,128]{3,1,2,0:T(8,128)} %copy.54) | copy-start | bytes 2359300
Sparse Core Ops, SparseCore 0:
  20.0 30.9 all-gather.3
  180.9 46.8 all-gather.7
  229.4 45.6 all-gather.5
Sparse Core Ops, SparseCore 1:
  84.9 85.6 all-reduce.2
  178.6 86.6 all-reduce.4
